TPU v7x, 256 devices: a whole 4x4x8 slice. The times are simulated.
256 devices in a mesh: cube: 8 (over x, y_lo), blk: 32 (over z, y_hi, core).
Axes of the slice: x: 4, y: 4 (y_hi: 2, y_lo: 2; y = y_hi * 2 + y_lo), z: 8, core: 2. Of those that a mesh axis runs over, the one named last changes fastest.
Arguments:
- updates: float32 [8, 32, 8, 128, 128], P('cube', 'blk'), may hold values from -6 to 6
- pivot_panel: float32 [16384, 256], P(('cube', 'blk')), may hold values from -1.5 to 1.5
- map_low: int32 [8, 32, 8], P('cube', 'blk'), may hold values from 0 to 7
- map_own: int32 [8, 32, 8], P('cube', 'blk'), may hold values from 0 to 63
- map_out: int32 [8, 32, 8], P('cube', 'blk'), may hold values from 0 to 63
Outputs:
- schur: float32 [8, 32, 64, 16384], P(None, 'blk', None, 'cube')
All inputs are finite; a program needn't handle non-finite values.
Results may differ from a plain program's by a relative error of at most 0.000058.
Values sent between devices are 32-bit elements; how exact they have to be, the bound alone decides.
A program may use at most 64 MiB of HBM per device.

v0:
```python
import jax
import jax.numpy as jnp
from jax import lax
from jax.sharding import PartitionSpec as P

exact_mode = lax.Precision.HIGHEST


def swapped(shard, axis, bit):
    return lax.ppermute(shard, axis, [(i, i ^ 1 << bit) for i in range(lax.axis_size(axis))])


def one_hot(targets, classes):
    return (targets[:, None] == jnp.arange(classes, dtype=jnp.int32)).astype(jnp.float32)


def scatter_slots(targets, classes, blocks):
    return jnp.dot(
        one_hot(targets, classes).T,
        blocks,
        precision=exact_mode,
        preferred_element_type=jnp.float32,
    )


def local(updates, pivot_panel, map_low, map_own, map_out):
    bit_count = lax.axis_size("cube").bit_length() - 1
    block_count = updates.shape[2]
    tile_size = updates.shape[3]
    part_rows = pivot_panel.shape[0]
    row_count = lax.axis_size("cube") * part_rows
    col_count = lax.axis_size("blk") * part_rows
    tile_count = row_count // tile_size * (col_count // tile_size)
    blocks = updates.reshape(block_count, tile_size * tile_size)
    low_targets = map_low.reshape(block_count)
    out_targets = map_out.reshape(block_count)
    outgoing = scatter_slots(low_targets, block_count, blocks)
    merged = blocks + swapped(outgoing, "cube", bit_count - 2)
    assembled = scatter_slots(map_own.reshape(block_count), tile_count, merged)
    peer_blocks, peer_map = swapped((merged, out_targets), "cube", bit_count - 1)
    assembled = assembled + scatter_slots(peer_map, tile_count, peer_blocks)
    row_panel = lax.all_gather(pivot_panel, "cube", axis=0, tiled=True)
    contribution = lax.dot_general(
        row_panel,
        lax.all_gather(pivot_panel, "blk", axis=0, tiled=True),
        (((1,), (1,)), ((), ())),
        precision=exact_mode,
        preferred_element_type=jnp.float32,
    )
    tile_grid = assembled.reshape(
        row_count // tile_size, col_count // tile_size, tile_size, tile_size
    )
    front_block = tile_grid.transpose(0, 2, 1, 3).reshape(row_count, col_count)
    schur_block = front_block - contribution
    return schur_block.reshape(lax.axis_size("cube"), 1, part_rows, col_count)


def solution(mesh):
    placed = (
        P("cube", "blk", None, None, None),
        P(("cube", "blk"), None),
        P("cube", "blk", None),
        P("cube", "blk", None),
        P("cube", "blk", None),
    )
    return jax.shard_map(
        local, mesh=mesh, in_specs=placed, out_specs=P(None, "blk", None, "cube"), check_vma=False
    )
```

profile of v0, /device:TPU:1, one launch (start us, length us, event | category | flops | bytes accessed | tf_op | source)
XLA Modules:
  0.0 110.4 jit_solution(16384519400459154841)
XLA Ops:
  6.5 0.0 copy-start
  6.5 0.0 all-gather.2.cloned.1.call-start
  6.5 1.8 %fusion.1 = f32[8,16384]{1,0:T(8,128)S(1)} fusion(f32[1,8,128,128]{3,2,1,0:T(8,128)} %bitcast.30, s32[8]{0:T(128)} %bitcast.32), kind=kOutput, calls=%fused_computation.5 | convolution fusion | flops 12582976 | bytes 1048608 | tf_op jit(solution)/shard_map/dot_general | solution.py:18
  8.3 2.1 %collective-permute-start = (f32[8,16384]{1,0:T(8,128)S(1)}, f32[8,16384]{1,0:T(8,128)S(1)}, u32[]{:S(2)}, u32[]{:S(2)}) collective-permute-start(f32[8,16384]{1,0:T(8,128)S(1)} %fusion.1), channel_id=1, source_target_pairs={{0,64},{32,96},{64,0},{96,32},{128,192},{160,224},{192,128},{224,1... | collective-permute-start | bytes 1572872 | tf_op jit(solution)/shard_map/ppermute | solution.py:10
  10.5 0.0 all-gather.2.cloned.1.call-update
  10.5 10.3 %collective-permute-done = f32[8,16384]{1,0:T(8,128)S(1)} collective-permute-done((f32[8,16384]{1,0:T(8,128)S(1)}, f32[8,16384]{1,0:T(8,128)S(1)}, u32[]{:S(2)}, u32[]{:S(2)}) %collective-permute-start) | collective-permute-done | bytes 524320 | tf_op jit(solution)/shard_map/ppermute | solution.py:10
  20.8 1.4 %bitcast_add_fusion = f32[8,16384]{1,0:T(8,128)S(1)} fusion(f32[8,16384]{1,0:T(8,128)S(1)} %collective-permute-done, f32[1,8,128,128]{3,2,1,0:T(8,128)} %bitcast.31), kind=kLoop, calls=%fused_computation.4 | loop fusion | flops 131072 | bytes 1572864 | tf_op jit(solution)/shard_map/add | solution.py:38
  22.1 4.1 %collective-permute-start.2 = (f32[8,16384]{1,0:T(8,128)S(1)}, f32[8,16384]{1,0:T(8,128)S(1)}, u32[]{:S(2)}, u32[]{:S(2)}) collective-permute-start(f32[8,16384]{1,0:T(8,128)S(1)} %bitcast_add_fusion), channel_id=1, source_target_pairs={{0,128},{32,160},{64,192},{96,224},{128,0},{160,32},{192,64},{224,... | collective-permute-start | bytes 1572872 | tf_op jit(solution)/shard_map/ppermute | solution.py:10
  26.2 0.1 collective-permute-start.1
  26.3 31.5 %all_gather.6 = f32[512,256]{1,0:T(8,128)S(1)} all-gather(f32[64,256]{1,0:T(8,128)} %param.6), channel_id=1, replica_groups=mesh['cube'=8,'blk'=32] {'cube'}, dimensions={0}, use_global_device_ids=true | all-gather | bytes 589824 | tf_op jit(solution)/shard_map/all_gather | solution.py:42
  57.8 0.0 collective-permute-done.1
  57.8 0.0 collective-permute-done.2
  57.8 1.9 %fusion.4 = f32[64,16384]{1,0:T(8,128)S(1)} fusion(f32[8,16384]{1,0:T(8,128)S(1)} %collective-permute-done.2, s32[8]{0:T(128)S(1)} %collective-permute-done.1), kind=kOutput, calls=%fused_computation.11 | convolution fusion | flops 100663808 | bytes 4718624 | tf_op jit(solution)/shard_map/dot_general | solution.py:18
  59.7 0.0 copy-done
  59.7 2.0 %fusion = f32[8,8,128,128]{3,1,2,0:T(8,128)S(1)} fusion(f32[64,16384]{1,0:T(8,128)S(1)} %fusion.4, f32[8,16384]{1,0:T(8,128)S(1)} %bitcast_add_fusion, s32[8]{0:T(128)S(1)} %bitcast.33), kind=kOutput, calls=%fused_computation.3 | convolution fusion | flops 101712384 | bytes 8912928 | tf_op jit(solution)/shard_map/dot_general | solution.py:18
  61.7 0.7 copy.9
  62.5 0.5 bitcast_bitcast_fusion
  63.0 4.4 %copy.6 = f32[4,128,16,128]{3,2,1,0:T(8,128)} copy(f32[4,128,16,128]{3,1,2,0:T(8,128)S(1)} %bitcast_bitcast_fusion) | data formatting | bytes 8388608 | tf_op jit(solution)/shard_map/transpose | solution.py:53
  67.4 27.2 %all-gather.2.cloned.1.call-done = f32[2048,256]{1,0:T(8,128)} async-done(((f32[64,256]{1,0:T(8,128)}), f32[2048,256]{1,0:T(8,128)}) %all-gather.2.cloned.1.call-update) | async-done | bytes 2097168 | tf_op jit(solution)/shard_map/all_gather | solution.py:45
  94.5 9.0 %bitcast_subtract_fusion = f32[512,2048]{1,0:T(8,128)} fusion(f32[64,8,16,128]{3,2,1,0:T(8,128)} %bitcast.28, f32[512,256]{1,0:T(8,128)S(1)} %all_gather.6, f32[2048,256]{1,0:T(8,128)} %all-gather.2.cloned.1.call-done), kind=kOutput, calls=%fused_computation.1 | convolution fusion | flops 3222274048 | bytes 11010048 | tf_op jit(solution)/shard_map/dot_general | solution.py:43
Async XLA Ops:
  6.5 53.2 %copy-start = (s32[1,1,8]{2,1,0:T(1,128)S(1)}, s32[1,1,8]{2,1,0:T(1,128)}, u32[]{:S(2)}) copy-start(s32[1,1,8]{2,1,0:T(1,128)} %param.8) | copy-start | bytes 100
  6.5 88.0 %all-gather.2.cloned.1.call-start = ((), (), s32[]{:S(2)}) async-start(), calls=%async_computation | async-start | bytes 2162688 | tf_op jit(solution)/shard_map/all_gather | solution.py:45
  8.3 12.4 %collective-permute-start = (f32[8,16384]{1,0:T(8,128)S(1)}, f32[8,16384]{1,0:T(8,128)S(1)}, u32[]{:S(2)}, u32[]{:S(2)}) collective-permute-start(f32[8,16384]{1,0:T(8,128)S(1)} %fusion.1), channel_id=1, source_target_pairs={{0,64},{32,96},{64,0},{96,32},{128,192},{160,224},{192,128},{224,1... | collective-permute-start | bytes 1572872 | tf_op jit(solution)/shard_map/ppermute | solution.py:10
  22.1 35.7 %collective-permute-start.2 = (f32[8,16384]{1,0:T(8,128)S(1)}, f32[8,16384]{1,0:T(8,128)S(1)}, u32[]{:S(2)}, u32[]{:S(2)}) collective-permute-start(f32[8,16384]{1,0:T(8,128)S(1)} %bitcast_add_fusion), channel_id=1, source_target_pairs={{0,128},{32,160},{64,192},{96,224},{128,0},{160,32},{192,64},{224,... | collective-permute-start | bytes 1572872 | tf_op jit(solution)/shard_map/ppermute | solution.py:10
  26.2 31.6 %collective-permute-start.1 = (s32[8]{0:T(128)}, s32[8]{0:T(128)S(1)}, u32[]{:S(2)}, u32[]{:S(2)}) collective-permute-start(s32[8]{0:T(128)} %bitcast.34), channel_id=1, source_target_pairs={{0,128},{32,160},{64,192},{96,224},{128,0},{160,32},{192,64},{224,... | collective-permute-start | bytes 104 | tf_op jit(solution)/shard_map/ppermute | solution.py:10
Sparse Core Ops, SparseCore 0:
  10.6 83.8 all-gather.1
where the time goes:
time: 111 us; the launch traced here: 110 us
  waiting for transfers between devices  37.5 us (34%)
  blocking collectives  31.5 us (28%)
  matrix products  14.7 us (13%)
  between operations  13.4 us (12%)
  starting transfers between devices  6.33 us (6%)
  local copies, waits for them, and re-layouts  5.61 us (5%)
  other arithmetic  1.36 us (1%)
    all_gather x1, blocking collectives, local(): row_panel = lax.all_gather(pivot_panel, 'cube', axis=0, tiled=True)  31.5 us
    all_gather x1, waiting for transfers between devices, local(): lax.all_gather(pivot_panel, 'blk', axis=0, tiled=True)  27.2 us
    ppermute x3, waiting for transfers between devices, swapped(): lax.ppermute(shard, axis, [(i, i ^ 1 << bit) for i in range(lax.axis_size...  10.3 us
    dot_general x1, matrix products, local(): lax.dot_general(row_panel, lax.all_gather(pivot_panel, 'blk', axis=0, til...  8.98 us
    ppermute x3, starting transfers between devices, swapped(): lax.ppermute(shard, axis, [(i, i ^ 1 << bit) for i in range(lax.axis_size...  6.33 us
    dot_general x3, matrix products, scatter_slots(): jnp.dot(one_hot(targets, classes).T, blocks, precision=exact_mode, prefer...  5.7 us
    transpose x2, local copies, waits for them, and re-layouts, local(): front_block = tile_grid.transpose(0, 2, 1, 3).reshape(row_count, col_count)  4.87 us
  transfers between devices with their start and end apart: 4, of which 2 were waited for; matrix products, arithmetic and copies ran while one was open for 10% of the time, Pallas kernels for 0%

commit v1 on v0

v1 whole, which is shorter than its diff:
```python
import functools

import jax
import jax.numpy as jnp
from jax import lax
from jax.experimental import pallas as pl
from jax.experimental.pallas import tpu as pltpu
from jax.sharding import PartitionSpec as P

MESH = pl.DeviceIdType.MESH
CHUNKS = 16
PIECES = 2


def flip(index, bit):
    return index + bit - 2 * bit * lax.rem(lax.div(index, bit), 2)


def exchange_kernel(
    updates,
    panel,
    map_low,
    map_own,
    map_out,
    own_u,
    peer_u,
    upper_u,
    product,
    places,
    rows,
    cols,
    left,
    outgoing,
    relay_u,
    relay_map,
    low_scalars,
    local_sem,
    row_send,
    row_recv,
    col_send,
    col_recv,
    pair_send,
    pair_recv,
    upd_send,
    upd_recv,
    map_send,
    map_recv,
):
    cube, blk = lax.axis_index("cube"), lax.axis_index("blk")
    z_count = lax.axis_size("blk") // 4
    blk_count = 4 * z_count
    slots, tile = own_u.shape[0], own_u.shape[1]
    part = panel.shape[0]

    low = {"cube": flip(cube, 2), "blk": blk}
    across = {"cube": flip(flip(cube, 2), 4), "blk": blk}
    y_pair = {"cube": flip(cube, 1), "blk": blk}
    y_other = {"cube": flip(cube, 1), "blk": flip(blk, 2)}
    z_up = {"cube": cube, "blk": lax.rem(blk + 4, blk_count)}
    z_down = {"cube": cube, "blk": lax.rem(blk + blk_count - 4, blk_count)}
    pair = {"cube": cube, "blk": flip(blk, 1)}

    in_flight = []

    def send(src, dst, sems, at, device):
        copy = pltpu.make_async_remote_copy(
            src_ref=src,
            dst_ref=dst,
            send_sem=sems[0].at[at],
            recv_sem=sems[1].at[at],
            device_id=device,
            device_id_type=MESH,
        )
        copy.start()
        in_flight.append(copy)

    def arrived(dst, sems, at):
        pltpu.make_async_remote_copy(
            src_ref=dst,
            dst_ref=dst,
            send_sem=sems[0].at[at],
            recv_sem=sems[1].at[at],
            device_id=low,
            device_id_type=MESH,
        ).wait_recv()

    row_sems, col_sems = (row_send, row_recv), (col_send, col_recv)
    pair_sems, upd_sems = (pair_send, pair_recv), (upd_send, upd_recv)
    map_sems = (map_send, map_recv)

    def span(piece):
        return pl.ds(piece * (part // PIECES), part // PIECES)

    barrier = pltpu.get_barrier_semaphore()
    everyone = (low, across, y_pair, y_other, z_up, z_down, pair)
    for device in everyone:
        pl.semaphore_signal(barrier, inc=1, device_id=device, device_id_type=MESH)

    here = [
        pltpu.make_async_copy(map_low.at[0, 0], low_scalars, local_sem.at[0]),
        pltpu.make_async_copy(updates.at[0, 0], own_u, local_sem.at[1]),
        pltpu.make_async_copy(panel, rows.at[cube], local_sem.at[2]),
        pltpu.make_async_copy(panel, cols.at[blk], local_sem.at[3]),
        pltpu.make_async_copy(map_own.at[0, 0], places.at[0], local_sem.at[4]),
    ]
    for copy in here:
        copy.start()
    pl.semaphore_wait(barrier, len(everyone))

    def row_at(message, piece):
        return message * PIECES + piece

    def chunk_rows(chunk):
        return pl.ds(chunk * (tile // CHUNKS), tile // CHUNKS)

    for piece in range(PIECES):
        mine = panel.at[span(piece)]
        there = rows.at[cube, span(piece)]
        send(mine, there, row_sems, row_at(0, piece), low)
        send(mine, there, row_sems, row_at(1, piece), across)
        send(mine, there, row_sems, row_at(2, piece), y_pair)

    half = z_count // 2
    per_direction = (half - 1) * PIECES + 1

    def z_at(kind, direction, distance, piece):
        step = (distance - 1) * PIECES + (piece if distance < half else 0)
        return 2 + (kind * 2 + direction) * per_direction + step

    def z_slot(kind, direction, distance):
        shift = 4 * distance
        base = blk if kind == 0 else flip(blk, 2)
        return lax.rem(base + (blk_count - shift if direction == 0 else shift), blk_count)

    z_devices = (z_up, z_down)
    for piece in range(PIECES):
        for direction in range(2):
            send(
                panel.at[span(piece)],
                cols.at[blk, span(piece)],
                col_sems,
                z_at(0, direction, 1, piece),
                z_devices[direction],
            )
    send(panel, cols.at[blk], pair_sems, 0, pair)
    send(map_low.at[0, 0], places.at[1], map_sems, 0, low)
    send(map_out.at[0, 0], relay_map.at[0, 0], map_sems, 1, low)
    for chunk in range(CHUNKS):
        send(
            updates.at[0, 0, :, chunk_rows(chunk)],
            peer_u.at[:, chunk_rows(chunk)],
            upd_sems,
            chunk,
            low,
        )

    here[0].wait()
    here[1].wait()
    targets = [low_scalars[slot] for slot in range(slots)]

    @pl.loop(0, tile // 8)
    def _(step):
        at = pl.ds(pl.multiple_of(step * 8, 8), 8)
        blocks = [own_u[slot, at] for slot in range(slots)]
        for target in range(slots):
            terms = [
                blocks[slot] * jnp.where(targets[slot] == target, 1.0, 0.0)
                for slot in range(slots)
            ]
            while len(terms) > 1:
                terms = [a + b for a, b in zip(terms[::2], terms[1::2])]
            outgoing[target, at] = terms[0]

    low_slot = flip(cube, 2)
    across_slot = flip(flip(cube, 2), 4)
    upper_slot = flip(cube, 4)
    y_slot = flip(cube, 1)

    def row_event(message, slot, piece, forwards):
        there = rows.at[slot, span(piece)]
        arrived(there, row_sems, row_at(message, piece))
        for next_message, device in forwards:
            send(there, there, row_sems, row_at(next_message, piece), device)

    def y_relay(piece):
        there = rows.at[y_slot, span(piece)]
        arrived(there, row_sems, row_at(2, piece))
        send(there, cols.at[blk, span(piece)], col_sems, piece, y_other)

    def y_far(piece):
        there = cols.at[flip(blk, 2), span(piece)]
        arrived(there, col_sems, piece)
        for direction in range(2):
            send(there, there, col_sems, z_at(1, direction, 1, piece), z_devices[direction])
        if piece == PIECES - 1:
            whole = cols.at[flip(blk, 2)]
            send(whole, whole, pair_sems, 1, pair)

    def pair_at(kind, direction, distance):
        return 2 + (kind * 2 + direction) * half + distance - 1

    def z_event(kind, direction, distance, piece):
        slot = z_slot(kind, direction, distance)
        there = cols.at[slot, span(piece)]
        arrived(there, col_sems, z_at(kind, direction, distance, piece))
        last = distance == half
        onward = distance + 1 < half or (distance + 1 == half and piece == direction)
        if onward:
            at = z_at(kind, direction, distance + 1, piece)
            send(there, there, col_sems, at, z_devices[direction])
        if last:
            send(there, there, pair_sems, pair_at(kind, direction, distance), pair)
        elif piece == PIECES - 1:
            whole = cols.at[slot]
            send(whole, whole, pair_sems, pair_at(kind, direction, distance), pair)

    def chunk_event(chunk):
        at = chunk_rows(chunk)
        arrived(peer_u.at[:, at], upd_sems, chunk)
        relay_u[:, at] = peer_u[:, at] + outgoing[:, at]
        if chunk == 0:
            arrived(relay_map.at[0, 0], map_sems, 1)
            send(relay_map.at[0, 0], places.at[2], map_sems, 2, across)
        send(relay_u.at[:, at], upper_u.at[:, at], upd_sems, CHUNKS + chunk, across)

    piece_time, hop_time = 0.7, 1.65
    events = []

    def when(time, event, *operands):
        events.append((time, len(events), functools.partial(event, *operands)))

    hop = hop_time + piece_time
    for piece in range(PIECES):
        late = piece * piece_time
        when(hop + late, y_relay, piece)
        when(hop + late, row_event, 0, low_slot, piece, ((3, across), (4, y_pair)))
        when(hop + late, row_event, 1, across_slot, piece, ((5, y_pair),))
        when(2 * hop + late, y_far, piece)
        when(2 * hop + late, row_event, 3, upper_slot, piece, ((6, y_pair),))
        for kind in range(2):
            for distance in range(1, half + 1):
                for direction in range(2):
                    if distance < half or piece == direction:
                        time = hop * (distance + 2 * kind) + late
                        when(time, z_event, kind, direction, distance, piece)
    for chunk in range(CHUNKS):
        when(hop + piece_time * (chunk + PIECES), chunk_event, chunk)
    for _, _, event in sorted(events, key=lambda entry: entry[:2]):
        event()

    for message, bit in ((4, 2), (5, 6), (6, 4)):
        slot = flip(y_slot, 2) if bit != 4 else flip(y_slot, 4)
        slot = flip(slot, 4) if bit == 6 else slot
        for piece in range(PIECES):
            arrived(rows.at[slot, span(piece)], row_sems, row_at(message, piece))
    here[2].wait()
    here[3].wait()
    here[4].wait()

    depth = panel.shape[1]
    row_count = rows.shape[0] * part
    values = -rows[...].reshape(row_count, depth)
    high = values.astype(jnp.bfloat16)
    rest = (values - high.astype(jnp.float32)).astype(jnp.bfloat16)
    left[:, 0:depth] = high
    left[:, depth : 2 * depth] = high
    left[:, 2 * depth : 3 * depth] = rest

    def other(slot):
        return flip(slot, 1)

    arrived(cols.at[other(blk)], pair_sems, 0)
    arrived(cols.at[other(flip(blk, 2))], pair_sems, 1)
    for kind in range(2):
        for distance in range(1, half):
            for direction in range(2):
                slot = other(z_slot(kind, direction, distance))
                arrived(cols.at[slot], pair_sems, pair_at(kind, direction, distance))

    here_z = lax.div(blk, 4)
    group = 4 * part

    def multiply(z):
        right = cols[pl.ds(z * 4, 4)].reshape(group, depth)
        high = right.astype(jnp.bfloat16)
        rest = (right - high.astype(jnp.float32)).astype(jnp.bfloat16)
        right = jnp.concatenate([high, rest, high], axis=1)
        at = pl.ds(pl.multiple_of(z * group, group), group)
        product[:, at] = lax.dot_general(
            left[...],
            right,
            (((1,), (1,)), ((), ())),
            preferred_element_type=jnp.float32,
        )

    @pl.loop(0, z_count - 1)
    def _(step):
        multiply(lax.rem(here_z + half + 1 + step, z_count))

    for kind in range(2):
        for direction in range(2):
            slot = other(z_slot(kind, direction, half))
            at = pair_at(kind, direction, half)
            arrived(cols.at[slot, span(direction)], pair_sems, at)
    multiply(lax.rem(here_z + half, z_count))

    arrived(places.at[1], map_sems, 0)
    arrived(places.at[2], map_sems, 2)
    for chunk in range(CHUNKS):
        arrived(upper_u.at[:, chunk_rows(chunk)], upd_sems, CHUNKS + chunk)
    for copy in in_flight:
        copy.wait_send()


def place_kernel(
    product, own_u, peer_u, upper_u, places, out, front, sems
):
    slots, tile = own_u.shape[0], own_u.shape[1]
    tile_rows, tile_cols = front.shape[0] // tile, front.shape[1] // tile
    copies = []
    for tile_row in range(tile_rows):
        rows = pl.ds(tile_row * tile, tile)
        front[rows] = product[rows]

        def add(target, source, slot):
            @pl.when(lax.div(target, tile_cols) == tile_row)
            def _():
                col = lax.rem(target, tile_cols) * tile
                at = pl.ds(pl.multiple_of(col, tile), tile)
                front[rows, at] += source[slot]

        @pl.loop(0, slots)
        def _(slot):
            add(places[0, slot], own_u, slot)
            add(places[0, places[1, slot]], peer_u, slot)
            add(places[2, slot], upper_u, slot)

        copy = pltpu.make_async_copy(front.at[rows], out.at[rows], sems.at[tile_row])
        copy.start()
        copies.append(copy)
    for copy in copies:
        copy.wait()


def in_hbm(array):
    return pltpu.with_memory_space_constraint(array, pltpu.HBM)


def local(updates, pivot_panel, map_low, map_own, map_out):
    slots, tile = updates.shape[2], updates.shape[3]
    part, depth = pivot_panel.shape
    cubes, blks = lax.axis_size("cube"), lax.axis_size("blk")
    row_count, col_count = cubes * part, blks * part
    z_count = blks // 4
    half = z_count // 2
    f32, i32, bf16 = jnp.float32, jnp.int32, jnp.bfloat16
    dma = pltpu.SemaphoreType.DMA
    hbm = pl.BlockSpec(memory_space=pltpu.HBM)
    vmem = pl.BlockSpec(memory_space=pltpu.VMEM)
    smem = pl.BlockSpec(memory_space=pltpu.SMEM)
    z_messages = 2 + 4 * ((half - 1) * PIECES + 1)
    pair_messages = 2 + 4 * half
    blocks = pltpu.VMEM((slots, tile, tile), f32)
    own_u, peer_u, upper_u, product, places = pl.pallas_call(
        exchange_kernel,
        out_shape=(
            blocks,
            blocks,
            blocks,
            pltpu.VMEM((row_count, col_count), f32),
            pltpu.VMEM((3, slots), i32),
        ),
        in_specs=[hbm] * 5,
        out_specs=(vmem,) * 5,
        scratch_shapes=[
            pltpu.VMEM((cubes, part, depth), f32),
            pltpu.VMEM((blks, part, depth), f32),
            pltpu.VMEM((row_count, 3 * depth), bf16),
            pltpu.VMEM((slots, tile, tile), f32),
            pltpu.VMEM((slots, tile, tile), f32),
            pltpu.VMEM((1, 1, slots), i32),
            pltpu.SMEM((slots,), i32),
            dma((5,)),
            dma((7 * PIECES,)),
            dma((7 * PIECES,)),
            dma((z_messages,)),
            dma((z_messages,)),
            dma((pair_messages,)),
            dma((pair_messages,)),
            dma((2 * CHUNKS,)),
            dma((2 * CHUNKS,)),
            dma((3,)),
            dma((3,)),
        ],
        compiler_params=pltpu.CompilerParams(
            collective_id=0, has_side_effects=True, vmem_limit_bytes=24 << 20
        ),
    )(*(in_hbm(array) for array in (updates, pivot_panel, map_low, map_own, map_out)))
    out = pl.pallas_call(
        place_kernel,
        out_shape=jax.ShapeDtypeStruct((row_count, col_count), f32),
        in_specs=[vmem] * 4 + [smem],
        out_specs=hbm,
        scratch_shapes=[pltpu.VMEM((row_count, col_count), f32), dma((row_count // tile,))],
        compiler_params=pltpu.CompilerParams(vmem_limit_bytes=16 << 20),
    )(product, own_u, peer_u, upper_u, places)
    return out.reshape(cubes, 1, part, col_count)


def solution(mesh):
    placed = (
        P("cube", "blk", None, None, None),
        P(("cube", "blk"), None),
        P("cube", "blk", None),
        P("cube", "blk", None),
        P("cube", "blk", None),
    )
    return jax.shard_map(
        local, mesh=mesh, in_specs=placed, out_specs=P(None, "blk", None, "cube"), check_vma=False
    )
```

time: 111 us -> 38.7 us (0.35)
  Pallas kernels: 0 us -> 38.6 us
  waiting for transfers between devices: 37.5 us -> 0 us
  blocking collectives: 31.5 us -> 0 us
  matrix products: 14.7 us -> 0 us
  between operations: 13.4 us -> 0.01 us
  starting transfers between devices: 6.33 us -> 0 us
  local copies, waits for them, and re-layouts: 5.61 us -> 0 us
  other arithmetic: 1.36 us -> 0 us
    pallas_call x0 -> x2, Pallas kernels: none -> 38.6 us  [the longest x1 35.1 us: local(): pl.pallas_call(exchange_kernel, out_shape=(blocks, blocks, blocks, pltpu....]
    all_gather x1 -> x0, blocking collectives: 31.5 us -> none  [local(): row_panel = lax.all_gather(pivot_panel, 'cube', axis=0, tiled=True)]
    all_gather x1 -> x0, waiting for transfers between devices: 27.2 us -> none  [local(): lax.all_gather(pivot_panel, 'blk', axis=0, tiled=True)]
    dot_general x4 -> x0, matrix products: 14.7 us -> none  [the longest x1 8.98 us: local(): lax.dot_general(row_panel, lax.all_gather(pivot_panel, 'blk', axis=0, til...]
    ppermute x3 -> x0, waiting for transfers between devices: 10.3 us -> none  [swapped(): lax.ppermute(shard, axis, [(i, i ^ 1 << bit) for i in range(lax.axis_size...]
    ppermute x3 -> x0, starting transfers between devices: 6.33 us -> none  [swapped(): lax.ppermute(shard, axis, [(i, i ^ 1 << bit) for i in range(lax.axis_size...]
    transpose x2 -> x0, local copies, waits for them, and re-layouts: 4.87 us -> none  [local(): front_block = tile_grid.transpose(0, 2, 1, 3).reshape(row_count, col_count)]
    add x1 -> x0, other arithmetic: 1.36 us -> none  [local(): merged = blocks + swapped(outgoing, 'cube', bit_count - 2)]
  transfers between devices with their start and end apart: 4 -> 0, of which waited for: 2 -> 0; matrix products, arithmetic and copies ran while one was open for 10% -> 0% of each run, Pallas kernels for 0% -> 0%
where the time goes in v1:
time: 38.7 us
  Pallas kernels  38.6 us (100%)
    pallas_call x1, Pallas kernels, local(): pl.pallas_call(exchange_kernel, out_shape=(blocks, blocks, blocks, pltpu....  35.1 us
    pallas_call x1, Pallas kernels, local(): pl.pallas_call(place_kernel, out_shape=jax.ShapeDtypeStruct((row_count, c...  3.58 us

profile of v1, /device:TPU:1, one launch (start us, length us, event | category | flops | bytes accessed | tf_op | source)
XLA Modules:
  0.0 38.7 jit_solution(18038798007540203880)
XLA Ops:
  0.0 35.1 %shard_map.55 = (f32[8,128,128]{2,1,0:T(8,128)S(1)}, f32[8,128,128]{2,1,0:T(8,128)S(1)}, f32[8,128,128]{2,1,0:T(8,128)S(1)}, f32[512,2048]{1,0:T(8,128)S(1)}, s32[3,8]{1,0:T(4,128)S(1)}) custom-call(f32[1,1,8,128,128]{4,3,2,1,0:T(8,128)} %updates.1, f32[64,256]{1,0:T(8,128)} %panel.1, s32[1,1,8]{2,1,0:T(1,128)} %map_low.1, s32[1,1,8]{2,1,0:T(1,128)} %map_own.1, ...), custom_call_target="tpu_custom_call" | custom-call | tf_op jit(solution)/shard_map/pallas_call | solution.py:364
  35.1 3.6 %shard_map.56 = f32[512,2048]{1,0:T(8,128)} custom-call(f32[512,2048]{1,0:T(8,128)S(1)} %get-tuple-element.10.product, f32[8,128,128]{2,1,0:T(8,128)S(1)} %get-tuple-element.11.own_u, f32[8,128,128]{2,1,0:T(8,128)S(1)} %get-tuple-element.12.peer_u, f32[8,128,128]{2,1,0:T(8,128)S(1)} %get-tuple-element.13.upper_u, s32[3,8]{1,0:T(4,128)S(1)} %get-tuple-element.14.places), custom_call_target="tpu_custom_call" | custom-call | tf_op jit(solution)/shard_map/pallas_call | solution.py:399

commit v2 on v1

--- a/solution.py
+++ b/solution.py
@@ -10,6 +10,10 @@
 MESH = pl.DeviceIdType.MESH
 CHUNKS = 16
 PIECES = 2
+FAR = 3
+X_STEP = 0.55
+Z_SHIFT = 0.0
+Z_STEP = 2.3
 
 
 def flip(index, bit):
@@ -55,7 +59,7 @@
     low = {"cube": flip(cube, 2), "blk": blk}
     across = {"cube": flip(flip(cube, 2), 4), "blk": blk}
     y_pair = {"cube": flip(cube, 1), "blk": blk}
-    y_other = {"cube": flip(cube, 1), "blk": flip(blk, 2)}
+    y_far = {"cube": cube, "blk": flip(blk, 2)}
     z_up = {"cube": cube, "blk": lax.rem(blk + 4, blk_count)}
     z_down = {"cube": cube, "blk": lax.rem(blk + blk_count - 4, blk_count)}
     pair = {"cube": cube, "blk": flip(blk, 1)}
@@ -92,7 +96,7 @@
         return pl.ds(piece * (part // PIECES), part // PIECES)
 
     barrier = pltpu.get_barrier_semaphore()
-    everyone = (low, across, y_pair, y_other, z_up, z_down, pair)
+    everyone = (low, across, y_pair, y_far, z_up, z_down, pair)
     for device in everyone:
         pl.semaphore_signal(barrier, inc=1, device_id=device, device_id_type=MESH)
 
@@ -142,6 +146,8 @@
                 z_at(0, direction, 1, piece),
                 z_devices[direction],
             )
+    for piece in range(PIECES):
+        send(panel.at[span(piece)], cols.at[blk, span(piece)], col_sems, piece, y_far)
     send(panel, cols.at[blk], pair_sems, 0, pair)
     send(map_low.at[0, 0], places.at[1], map_sems, 0, low)
     send(map_out.at[0, 0], relay_map.at[0, 0], map_sems, 1, low)
@@ -182,12 +188,7 @@
         for next_message, device in forwards:
             send(there, there, row_sems, row_at(next_message, piece), device)
 
-    def y_relay(piece):
-        there = rows.at[y_slot, span(piece)]
-        arrived(there, row_sems, row_at(2, piece))
-        send(there, cols.at[blk, span(piece)], col_sems, piece, y_other)
-
-    def y_far(piece):
+    def far_event(piece):
         there = cols.at[flip(blk, 2), span(piece)]
         arrived(there, col_sems, piece)
         for direction in range(2):
@@ -205,6 +206,10 @@
         arrived(there, col_sems, z_at(kind, direction, distance, piece))
         last = distance == half
         onward = distance + 1 < half or (distance + 1 == half and piece == direction)
+        if kind == 1 and distance + 1 >= FAR:
+            onward = False
+        if kind == 0 and distance >= FAR:
+            send(there, there, col_sems, z_at(1, direction, distance, piece), y_far)
         if onward:
             at = z_at(kind, direction, distance + 1, piece)
             send(there, there, col_sems, at, z_devices[direction])
@@ -223,31 +228,31 @@
             send(relay_map.at[0, 0], places.at[2], map_sems, 2, across)
         send(relay_u.at[:, at], upper_u.at[:, at], upd_sems, CHUNKS + chunk, across)
 
-    piece_time, hop_time = 0.7, 1.65
     events = []
 
     def when(time, event, *operands):
         events.append((time, len(events), functools.partial(event, *operands)))
 
-    hop = hop_time + piece_time
+    hop = 2.0 + X_STEP
     for piece in range(PIECES):
-        late = piece * piece_time
-        when(hop + late, y_relay, piece)
+        late = piece * X_STEP
         when(hop + late, row_event, 0, low_slot, piece, ((3, across), (4, y_pair)))
         when(hop + late, row_event, 1, across_slot, piece, ((5, y_pair),))
-        when(2 * hop + late, y_far, piece)
         when(2 * hop + late, row_event, 3, upper_slot, piece, ((6, y_pair),))
+        when(Z_SHIFT + 3.0 + late, far_event, piece)
         for kind in range(2):
             for distance in range(1, half + 1):
                 for direction in range(2):
                     if distance < half or piece == direction:
-                        time = hop * (distance + 2 * kind) + late
+                        time = Z_SHIFT + Z_STEP * distance + 3.0 * kind + late
                         when(time, z_event, kind, direction, distance, piece)
     for chunk in range(CHUNKS):
-        when(hop + piece_time * (chunk + PIECES), chunk_event, chunk)
+        when(2.0 + X_STEP * (chunk + 1 + PIECES), chunk_event, chunk)
     for _, _, event in sorted(events, key=lambda entry: entry[:2]):
         event()
 
+    for piece in range(PIECES):
+        arrived(rows.at[y_slot, span(piece)], row_sems, row_at(2, piece))
     for message, bit in ((4, 2), (5, 6), (6, 4)):
         slot = flip(y_slot, 2) if bit != 4 else flip(y_slot, 4)
         slot = flip(slot, 4) if bit == 6 else slot

time: 38.7 us -> 34.8 us (0.90)
  Pallas kernels: 38.6 us -> 34.7 us
    pallas_call x1, Pallas kernels: 35.1 us -> 31.1 us  [local(): pl.pallas_call(exchange_kernel, out_shape=(blocks, blocks, blocks, pltpu....]
where the time goes in v2:
time: 34.8 us; the launch traced here: 34.7 us
  Pallas kernels  34.7 us (100%)
    pallas_call x1, Pallas kernels, local(): pl.pallas_call(exchange_kernel, out_shape=(blocks, blocks, blocks, pltpu....  31.1 us
    pallas_call x1, Pallas kernels, local(): pl.pallas_call(place_kernel, out_shape=jax.ShapeDtypeStruct((row_count, c...  3.58 us

profile of v2, /device:TPU:1, one launch (start us, length us, event | category | flops | bytes accessed | tf_op | source)
XLA Modules:
  0.0 34.7 jit_solution(6123324466547267440)
XLA Ops:
  0.0 31.1 %shard_map.55 = (f32[8,128,128]{2,1,0:T(8,128)S(1)}, f32[8,128,128]{2,1,0:T(8,128)S(1)}, f32[8,128,128]{2,1,0:T(8,128)S(1)}, f32[512,2048]{1,0:T(8,128)S(1)}, s32[3,8]{1,0:T(4,128)S(1)}) custom-call(f32[1,1,8,128,128]{4,3,2,1,0:T(8,128)} %updates.1, f32[64,256]{1,0:T(8,128)} %panel.1, s32[1,1,8]{2,1,0:T(1,128)} %map_low.1, s32[1,1,8]{2,1,0:T(1,128)} %map_own.1, ...), custom_call_target="tpu_custom_call" | custom-call | tf_op jit(solution)/shard_map/pallas_call | solution.py:369
  31.1 3.6 %shard_map.56 = f32[512,2048]{1,0:T(8,128)} custom-call(f32[512,2048]{1,0:T(8,128)S(1)} %get-tuple-element.10.product, f32[8,128,128]{2,1,0:T(8,128)S(1)} %get-tuple-element.11.own_u, f32[8,128,128]{2,1,0:T(8,128)S(1)} %get-tuple-element.12.peer_u, f32[8,128,128]{2,1,0:T(8,128)S(1)} %get-tuple-element.13.upper_u, s32[3,8]{1,0:T(4,128)S(1)} %get-tuple-element.14.places), custom_call_target="tpu_custom_call" | custom-call | tf_op jit(solution)/shard_map/pallas_call | solution.py:404

commit v3 on v2

--- a/solution.py
+++ b/solution.py
@@ -8,12 +8,14 @@
 from jax.sharding import PartitionSpec as P
 
 MESH = pl.DeviceIdType.MESH
-CHUNKS = 16
+CHUNKS = 8
 PIECES = 2
 FAR = 3
 X_STEP = 0.55
 Z_SHIFT = 0.0
 Z_STEP = 2.3
+B_OFF = 3.0
+X_OFF = 2.0
 
 
 def flip(index, bit):
@@ -235,19 +237,19 @@
 
     hop = 2.0 + X_STEP
     for piece in range(PIECES):
-        late = piece * X_STEP
+        late = piece * X_STEP * 2 / PIECES
         when(hop + late, row_event, 0, low_slot, piece, ((3, across), (4, y_pair)))
         when(hop + late, row_event, 1, across_slot, piece, ((5, y_pair),))
         when(2 * hop + late, row_event, 3, upper_slot, piece, ((6, y_pair),))
-        when(Z_SHIFT + 3.0 + late, far_event, piece)
+        when(Z_SHIFT + B_OFF + late, far_event, piece)
         for kind in range(2):
             for distance in range(1, half + 1):
                 for direction in range(2):
                     if distance < half or piece == direction:
-                        time = Z_SHIFT + Z_STEP * distance + 3.0 * kind + late
+                        time = Z_SHIFT + Z_STEP * distance + B_OFF * kind + late
                         when(time, z_event, kind, direction, distance, piece)
     for chunk in range(CHUNKS):
-        when(2.0 + X_STEP * (chunk + 1 + PIECES), chunk_event, chunk)
+        when(X_OFF + X_STEP * (PIECES + (chunk + 1) * 16 / CHUNKS), chunk_event, chunk)
     for _, _, event in sorted(events, key=lambda entry: entry[:2]):
         event()
 
@@ -273,14 +275,6 @@
 
     def other(slot):
         return flip(slot, 1)
-
-    arrived(cols.at[other(blk)], pair_sems, 0)
-    arrived(cols.at[other(flip(blk, 2))], pair_sems, 1)
-    for kind in range(2):
-        for distance in range(1, half):
-            for direction in range(2):
-                slot = other(z_slot(kind, direction, distance))
-                arrived(cols.at[slot], pair_sems, pair_at(kind, direction, distance))
 
     here_z = lax.div(blk, 4)
     group = 4 * part
@@ -298,9 +292,24 @@
             preferred_element_type=jnp.float32,
         )
 
-    @pl.loop(0, z_count - 1)
+    def pairs_arrived(distance):
+        for kind in range(2):
+            for direction in range(2):
+                slot = other(z_slot(kind, direction, distance))
+                arrived(cols.at[slot], pair_sems, pair_at(kind, direction, distance))
+
+    arrived(cols.at[other(blk)], pair_sems, 0)
+    arrived(cols.at[other(flip(blk, 2))], pair_sems, 1)
+    for distance in range(1, half - 1):
+        pairs_arrived(distance)
+
+    @pl.loop(0, z_count - 3)
     def _(step):
-        multiply(lax.rem(here_z + half + 1 + step, z_count))
+        multiply(lax.rem(here_z + half + 2 + step, z_count))
+
+    pairs_arrived(half - 1)
+    for shift in (half + 1, half - 1):
+        multiply(lax.rem(here_z + shift, z_count))
 
     for kind in range(2):
         for direction in range(2):
@@ -317,29 +326,24 @@
         copy.wait_send()
 
 
-def place_kernel(
-    product, own_u, peer_u, upper_u, places, out, front, sems
-):
+def place_kernel(product, own_u, peer_u, upper_u, places, front, out, sems):
     slots, tile = own_u.shape[0], own_u.shape[1]
     tile_rows, tile_cols = front.shape[0] // tile, front.shape[1] // tile
+
+    def add(target, blocks, slot):
+        row = pl.multiple_of(lax.div(target, tile_cols) * tile, tile)
+        col = pl.multiple_of(lax.rem(target, tile_cols) * tile, tile)
+        front[pl.ds(row, tile), pl.ds(col, tile)] += blocks[slot]
+
+    @pl.loop(0, slots)
+    def _(slot):
+        add(places[0, slot], own_u, slot)
+        add(places[0, places[1, slot]], peer_u, slot)
+        add(places[2, slot], upper_u, slot)
+
     copies = []
     for tile_row in range(tile_rows):
         rows = pl.ds(tile_row * tile, tile)
-        front[rows] = product[rows]
-
-        def add(target, source, slot):
-            @pl.when(lax.div(target, tile_cols) == tile_row)
-            def _():
-                col = lax.rem(target, tile_cols) * tile
-                at = pl.ds(pl.multiple_of(col, tile), tile)
-                front[rows, at] += source[slot]
-
-        @pl.loop(0, slots)
-        def _(slot):
-            add(places[0, slot], own_u, slot)
-            add(places[0, places[1, slot]], peer_u, slot)
-            add(places[2, slot], upper_u, slot)
-
         copy = pltpu.make_async_copy(front.at[rows], out.at[rows], sems.at[tile_row])
         copy.start()
         copies.append(copy)
@@ -401,12 +405,16 @@
             collective_id=0, has_side_effects=True, vmem_limit_bytes=24 << 20
         ),
     )(*(in_hbm(array) for array in (updates, pivot_panel, map_low, map_own, map_out)))
-    out = pl.pallas_call(
+    _, out = pl.pallas_call(
         place_kernel,
-        out_shape=jax.ShapeDtypeStruct((row_count, col_count), f32),
+        out_shape=(
+            pltpu.VMEM((row_count, col_count), f32),
+            jax.ShapeDtypeStruct((row_count, col_count), f32),
+        ),
         in_specs=[vmem] * 4 + [smem],
-        out_specs=hbm,
-        scratch_shapes=[pltpu.VMEM((row_count, col_count), f32), dma((row_count // tile,))],
+        out_specs=(vmem, hbm),
+        scratch_shapes=[dma((row_count // tile,))],
+        input_output_aliases={0: 0},
         compiler_params=pltpu.CompilerParams(vmem_limit_bytes=16 << 20),
     )(product, own_u, peer_u, upper_u, places)
     return out.reshape(cubes, 1, part, col_count)

time: 34.8 us -> 33.1 us (0.951)
  Pallas kernels: 34.7 us -> 33 us
    pallas_call x1, Pallas kernels: 31.1 us -> 30 us  [local(): pl.pallas_call(exchange_kernel, out_shape=(blocks, blocks, blocks, pltpu....]
    pallas_call x1, Pallas kernels: 3.58 us -> 2.96 us  [local(): pl.pallas_call(place_kernel, out_shape=(pltpu.VMEM((row_count, col_count)...]
where the time goes in v3:
time: 33.1 us; the launch traced here: 33 us
  Pallas kernels  33 us (100%)
    pallas_call x1, Pallas kernels, local(): pl.pallas_call(exchange_kernel, out_shape=(blocks, blocks, blocks, pltpu....  30 us
    pallas_call x1, Pallas kernels, local(): pl.pallas_call(place_kernel, out_shape=(pltpu.VMEM((row_count, col_count)...  2.96 us

profile of v3, /device:TPU:1, one launch (start us, length us, event | category | flops | bytes accessed | tf_op | source)
XLA Modules:
  0.0 33.0 jit_solution(12959616198268469767)
XLA Ops:
  0.0 30.0 %shard_map.55 = (f32[8,128,128]{2,1,0:T(8,128)S(1)}, f32[8,128,128]{2,1,0:T(8,128)S(1)}, f32[8,128,128]{2,1,0:T(8,128)S(1)}, f32[512,2048]{1,0:T(8,128)S(1)}, s32[3,8]{1,0:T(4,128)S(1)}) custom-call(f32[1,1,8,128,128]{4,3,2,1,0:T(8,128)} %updates.1, f32[64,256]{1,0:T(8,128)} %panel.1, s32[1,1,8]{2,1,0:T(1,128)} %map_low.1, s32[1,1,8]{2,1,0:T(1,128)} %map_own.1, ...), custom_call_target="tpu_custom_call" | custom-call | tf_op jit(solution)/shard_map/pallas_call | solution.py:373
  30.1 3.0 %shard_map.56 = (f32[512,2048]{1,0:T(8,128)S(1)}, f32[512,2048]{1,0:T(8,128)}) custom-call(f32[512,2048]{1,0:T(8,128)S(1)} %get-tuple-element.11.product, f32[8,128,128]{2,1,0:T(8,128)S(1)} %get-tuple-element.12.own_u, f32[8,128,128]{2,1,0:T(8,128)S(1)} %get-tuple-element.13.peer_u, ...), custom_call_target="tpu_custom_call", output_to_operand_aliasing={{0}: (0, {})} | custom-call | tf_op jit(solution)/shard_map/pallas_call | solution.py:408

commit v4 on v3

--- a/solution.py
+++ b/solution.py
@@ -15,7 +15,7 @@
 Z_SHIFT = 0.0
 Z_STEP = 2.3
 B_OFF = 3.0
-X_OFF = 2.0
+X_OFF = 2.5
 
 
 def flip(index, bit):
@@ -120,12 +120,7 @@
         return pl.ds(chunk * (tile // CHUNKS), tile // CHUNKS)
 
     for piece in range(PIECES):
-        mine = panel.at[span(piece)]
-        there = rows.at[cube, span(piece)]
-        send(mine, there, row_sems, row_at(0, piece), low)
-        send(mine, there, row_sems, row_at(1, piece), across)
-        send(mine, there, row_sems, row_at(2, piece), y_pair)
-
+        send(panel.at[span(piece)], cols.at[blk, span(piece)], col_sems, piece, y_far)
     half = z_count // 2
     per_direction = (half - 1) * PIECES + 1
 
@@ -149,7 +144,11 @@
                 z_devices[direction],
             )
     for piece in range(PIECES):
-        send(panel.at[span(piece)], cols.at[blk, span(piece)], col_sems, piece, y_far)
+        mine = panel.at[span(piece)]
+        there = rows.at[cube, span(piece)]
+        send(mine, there, row_sems, row_at(0, piece), low)
+        send(mine, there, row_sems, row_at(1, piece), across)
+        send(mine, there, row_sems, row_at(2, piece), y_pair)
     send(panel, cols.at[blk], pair_sems, 0, pair)
     send(map_low.at[0, 0], places.at[1], map_sems, 0, low)
     send(map_out.at[0, 0], relay_map.at[0, 0], map_sems, 1, low)
@@ -208,9 +207,9 @@
         arrived(there, col_sems, z_at(kind, direction, distance, piece))
         last = distance == half
         onward = distance + 1 < half or (distance + 1 == half and piece == direction)
-        if kind == 1 and distance + 1 >= FAR:
+        if kind == 1 and distance + 1 >= (3, 2)[direction]:
             onward = False
-        if kind == 0 and distance >= FAR:
+        if kind == 0 and distance >= (3, 2)[direction]:
             send(there, there, col_sems, z_at(1, direction, distance, piece), y_far)
         if onward:
             at = z_at(kind, direction, distance + 1, piece)
@@ -335,8 +334,7 @@
         col = pl.multiple_of(lax.rem(target, tile_cols) * tile, tile)
         front[pl.ds(row, tile), pl.ds(col, tile)] += blocks[slot]
 
-    @pl.loop(0, slots)
-    def _(slot):
+    for slot in range(slots):
         add(places[0, slot], own_u, slot)
         add(places[0, places[1, slot]], peer_u, slot)
         add(places[2, slot], upper_u, slot)

time: 33.1 us -> 33 us (level)
  no operation moved by 1% of the time
where the time goes in v4:
time: 33 us; the launch traced here: 32.9 us
  Pallas kernels  32.9 us (100%)
    pallas_call x1, Pallas kernels, local(): pl.pallas_call(exchange_kernel, out_shape=(blocks, blocks, blocks, pltpu....  30 us
    pallas_call x1, Pallas kernels, local(): pl.pallas_call(place_kernel, out_shape=(pltpu.VMEM((row_count, col_count)...  2.95 us

profile of v4, /device:TPU:1, one launch (start us, length us, event | category | flops | bytes accessed | tf_op | source)
XLA Modules:
  0.0 32.9 jit_solution(1279375621958719822)
XLA Ops:
  0.0 30.0 %shard_map.55 = (f32[8,128,128]{2,1,0:T(8,128)S(1)}, f32[8,128,128]{2,1,0:T(8,128)S(1)}, f32[8,128,128]{2,1,0:T(8,128)S(1)}, f32[512,2048]{1,0:T(8,128)S(1)}, s32[3,8]{1,0:T(4,128)S(1)}) custom-call(f32[1,1,8,128,128]{4,3,2,1,0:T(8,128)} %updates.1, f32[64,256]{1,0:T(8,128)} %panel.1, s32[1,1,8]{2,1,0:T(1,128)} %map_low.1, s32[1,1,8]{2,1,0:T(1,128)} %map_own.1, ...), custom_call_target="tpu_custom_call" | custom-call | tf_op jit(solution)/shard_map/pallas_call | solution.py:371
  30.0 3.0 %shard_map.56 = (f32[512,2048]{1,0:T(8,128)S(1)}, f32[512,2048]{1,0:T(8,128)}) custom-call(f32[512,2048]{1,0:T(8,128)S(1)} %get-tuple-element.11.product, f32[8,128,128]{2,1,0:T(8,128)S(1)} %get-tuple-element.12.own_u, f32[8,128,128]{2,1,0:T(8,128)S(1)} %get-tuple-element.13.peer_u, ...), custom_call_target="tpu_custom_call", output_to_operand_aliasing={{0}: (0, {})} | custom-call | tf_op jit(solution)/shard_map/pallas_call | solution.py:406
